TPU v7x, 32 devices: a whole 2x2x4 slice. The times are simulated.
32 devices in a mesh: seq: 8 (over z, y), exp: 4 (over x, core).
Axes of the slice: x: 2, y: 2, z: 4, core: 2. Of those that a mesh axis runs over, the one named last changes fastest.
Arguments:
- projected: bfloat16 [4096, 3, 8192], P('seq', None, 'exp'), may hold values from -6 to 6
- log_decay: float32 [4096, 64], P('seq', 'exp'), may hold values from -2.5 to 0, as said below
- norm_gain: float32 [8192], P('exp'), may hold values from 0.1 to 1.9
- moe_tokens: bfloat16 [256, 6144], P(('seq', 'exp')), may hold values from -6 to 6
- expert_ids: int32 [256, 2], P(('seq', 'exp')), may hold values from 0 to 3, all different within a row; in each aligned block of 8 rows (0 to 7, 8 to 15, ...) at most 4 rows name the same one
- route_probs: float32 [256, 2], P(('seq', 'exp')), may hold values from 0.1 to 1
- w_in: bfloat16 [4, 6144, 2, 4608], P('exp', None, None, 'seq'), may hold values from -0.078125 to 0.078125
- w_out: bfloat16 [4, 4608, 6144], P('exp', 'seq'), may hold values from -0.09375 to 0.09375
Outputs:
- attn_out: bfloat16 [4096, 8192], P('seq', 'exp')
- moe_out: bfloat16 [256, 6144], P(('seq', 'exp'))
Inputs may be any that keep to these rules, and one draw needn't show every extreme that they name: `log_decay`: negative in every entry. `expert_ids`: A token names 2 different experts. In the rows of one device (aligned blocks of 8 tokens) no expert is named more than 4 times, a bound that some block reaches.
All inputs are finite; a program needn't handle non-finite values.
Results may differ from a plain program's by a relative error of at most 0.025.
Values may be sent and summed in bfloat16 or wider, within the bound.
No kernel may reach another device: no remote copies, remote signals or barrier semaphores. Data moves between devices by JAX's collectives and lax.ppermute only.
A program may use at most 128 MiB of HBM per device.

v0:
```python
import jax
import jax.numpy as jnp
from jax import lax
from jax.sharding import PartitionSpec as P

CAP = 4
EPS = 1e-06
HIGH = lax.Precision.HIGHEST


def prefix(shard, axis, join, neutral):
    place = lax.axis_index(axis)
    gathered = jax.tree.map(
        lambda a, kind: lax.all_gather(a.astype(kind), axis), shard, (jnp.bfloat16, jnp.bfloat16)
    )
    state = jax.tree.map(lambda a, e: jnp.zeros_like(a) + jnp.asarray(e, a.dtype), shard, neutral)

    def one(turn, state):
        return join(
            state,
            jax.tree.map(
                lambda a, own: lax.dynamic_index_in_dim(a, turn, 0, False).astype(own.dtype),
                gathered,
                shard,
            ),
        )

    return lax.fori_loop(0, place, one, state)


def combine_states(earlier, later):
    return (earlier[0] * later[0], later[0][:, None, None] * earlier[1] + later[1])


def on_device(projected, log_decay, norm_gain, moe_tokens, expert_ids, route_probs, w_in, w_out):
    rows = projected.shape[0]
    heads = log_decay.shape[1]
    width = projected.shape[2] // heads
    queries = projected[:, 0].reshape(rows, heads, width)
    key_rows = projected[:, 1].reshape(rows, heads, width)
    values = projected[:, 2].reshape(rows, heads, width)
    running = jnp.cumsum(log_decay, axis=0)
    last = running[-1]
    weighted = key_rows.astype(jnp.float32) * jnp.exp(last[None] - running)[:, :, None]
    block_state = jnp.einsum("thi,thj->hij", weighted, values.astype(jnp.float32), precision=HIGH)
    identity = (jnp.ones_like(last), jnp.zeros_like(block_state))
    _, carried = prefix((jnp.exp(last), block_state), "seq", combine_states, identity)
    scores = jnp.einsum("thd,uhd->htu", queries, key_rows, preferred_element_type=jnp.float32)
    turned = running.T
    gap = turned[:, :, None] - turned[:, None, :]
    causal = (jnp.arange(rows)[:, None] >= jnp.arange(rows)[None, :])[None]
    decay = jnp.exp(jnp.where(causal, gap, -jnp.inf))
    weights = (scores * decay).astype(jnp.bfloat16)
    local_part = jnp.einsum("htu,uhd->thd", weights, values, preferred_element_type=jnp.float32)
    carried_part = jnp.einsum(
        "thd,hde->the",
        queries.astype(jnp.float32) * jnp.exp(running)[:, :, None],
        carried,
        precision=HIGH,
    )
    mixed = local_part + carried_part
    scaled = mixed * lax.rsqrt(jnp.mean(mixed * mixed, axis=-1, keepdims=True) + EPS)
    attn_out = (scaled.reshape(rows, heads * width) * norm_gain).astype(jnp.bfloat16)
    count_tok = moe_tokens.shape[0]
    model_width = moe_tokens.shape[1]
    topk = expert_ids.shape[1]
    experts = w_in.shape[0] * lax.axis_size("exp")
    assigned = expert_ids.reshape(-1)
    onehot = (assigned[:, None] == jnp.arange(experts, dtype=jnp.int32)[None]).astype(jnp.int32)
    slot = jnp.sum((jnp.cumsum(onehot, axis=0) - onehot) * onehot, axis=1)
    target = assigned * CAP + slot
    pick = (target[None, :] == jnp.arange(experts * CAP, dtype=jnp.int32)[:, None]).astype(
        jnp.bfloat16
    )
    local_units = w_in.shape[3]
    joined_in = w_in.reshape(model_width, 2 * local_units)
    down = w_out[0]
    spread_rows = jnp.repeat(moe_tokens, topk, axis=0)
    outgoing = (
        jnp.dot(pick, spread_rows, preferred_element_type=jnp.float32)
        .astype(jnp.bfloat16)
        .reshape(experts, CAP, model_width)
    )
    arrived = lax.all_to_all(outgoing, "exp", split_axis=0, concat_axis=0, tiled=True)
    both = jnp.dot(
        lax.all_gather(arrived.reshape(experts * CAP, model_width), "seq", axis=0, tiled=True),
        joined_in,
        preferred_element_type=jnp.float32,
    )
    hidden = (jax.nn.silu(both[:, :local_units]) * both[:, local_units:]).astype(jnp.bfloat16)
    summed = lax.psum_scatter(
        jnp.dot(hidden, down, preferred_element_type=jnp.float32).astype(jnp.bfloat16),
        "seq",
        scatter_dimension=0,
        tiled=True,
    )
    results = summed.reshape(experts, CAP, model_width)
    returned = lax.all_to_all(results, "exp", split_axis=0, concat_axis=0, tiled=True)
    picked = jnp.dot(
        pick.T, returned.reshape(experts * CAP, model_width), preferred_element_type=jnp.float32
    )
    scaled_rows = picked * route_probs.reshape(-1)[:, None]
    moe_out = jnp.sum(scaled_rows.reshape(count_tok, topk, model_width), axis=1).astype(
        jnp.bfloat16
    )
    return (attn_out, moe_out)


def solution(mesh):
    in_specs = (
        P("seq", None, "exp"),
        P("seq", "exp"),
        P("exp"),
        P(("seq", "exp"), None),
        P(("seq", "exp"), None),
        P(("seq", "exp"), None),
        P("exp", None, None, "seq"),
        P("exp", "seq", None),
    )
    out_specs = (P("seq", "exp"), P(("seq", "exp"), None))
    return jax.shard_map(
        on_device, mesh=mesh, in_specs=in_specs, out_specs=out_specs, check_vma=False
    )
```

profile of v0, /device:TPU:31, one launch (start us, length us, event | category | flops | bytes accessed | tf_op | source)
XLA Modules:
  0.0 248.3 jit_solution(5509535321156864374)
XLA Ops:
  9.7 6.6 %all_to_all.10 = bf16[4,4,6144]{2,1,0:T(4,128)(2,1)S(1)} all-to-all(bf16[4,4,6144]{2,1,0:T(4,128)(2,1)S(1)} %reshape.109), channel_id=1, replica_groups=mesh['seq'=8,'exp'=4] {'exp'}, dimensions={0} | all-to-all | bytes 393216 | tf_op jit(solution)/shard_map/all_to_all | solution.py:84
  17.1 43.5 %all-gather.5.cloned.1.call-done = bf16[128,6144]{1,0:T(8,128)(2,1)} async-done(((bf16[16,6144]{1,0:T(8,128)(2,1)}), bf16[128,6144]{1,0:T(8,128)(2,1)}) %all-gather.5.cloned.1.call-update) | async-done | bytes 1572880 | tf_op jit(solution)/shard_map/all_gather | solution.py:86
  60.6 10.1 %fusion.26 = f32[128,1152]{1,0:T(8,128)S(1)} fusion(bf16[128,6144]{1,0:T(8,128)(2,1)} %all-gather.5.cloned.1.call-done, bf16[6144,1152]{0,1:T(8,128)(2,1)} %bitcast.59), kind=kOutput, calls=%fused_computation.47 | convolution fusion | flops 1811939328 | bytes 16318464 | tf_op jit(solution)/shard_map/dot_general | solution.py:85
  70.8 5.6 %convolution_convert_fusion = bf16[128,6144]{1,0:T(8,128)(2,1)} fusion(bf16[1,576,6144]{2,1,0:T(8,128)(2,1)} %param.17, f32[128,1152]{1,0:T(8,128)S(1)} %fusion.26), kind=kOutput, calls=%fused_computation.3 | convolution fusion | flops 907198464 | bytes 9306112 | tf_op jit(solution)/shard_map/dot_general | solution.py:92
  77.8 5.8 %fusion.25 = (bf16[512,1,2048]{2,0,1:T(8,128)(2,1)}, bf16[512,1,2048]{2,0,1:T(8,128)(2,1)}, bf16[512,1,2048]{2,0,1:T(8,128)(2,1)S(1)}) fusion(bf16[512,3,2048]{2,0,1:T(8,128)(2,1)} %param.10), kind=kLoop, calls=%fused_computation.46 | loop fusion | bytes 12582912 | tf_op jit(solution)/shard_map/slice | solution.py:40
  83.7 3.9 %copy.75 = bf16[512,1,2048]{0,2,1:T(8,128)(2,1)} copy(bf16[512,1,2048]{2,0,1:T(8,128)(2,1)} %get-tuple-element.57) | data formatting | bytes 4194304
  87.6 2.5 %copy.61 = bf16[512,1,2048]{0,2,1:T(8,128)(2,1)} copy(bf16[512,1,2048]{2,0,1:T(8,128)(2,1)S(1)} %get-tuple-element.59) | data formatting | bytes 4194304 | tf_op jit(solution)/shard_map/slice | solution.py:41
  90.5 5.3 %fusion.12 = bf16[16,128,128]{2,1,0:T(8,128)(2,1)} fusion(bf16[512,16,128]{0,2,1:T(8,128)(2,1)} %bitcast.64, bf16[512,16,128]{0,2,1:T(8,128)(2,1)} %bitcast.62, f32[512,16]{0,1:T(8,128)S(1)} %get-tuple-element.61), kind=kOutput, calls=%fused_computation.20 | convolution fusion | flops 1612972032 | bytes 4751360 | tf_op jit(solution)/shard_map/thi,thj->hij/dot_general | solution.py:45
  95.8 2.9 %copy.74 = bf16[512,1,2048]{0,2,1:T(8,128)(2,1)S(1)} copy(bf16[512,1,2048]{2,0,1:T(8,128)(2,1)} %get-tuple-element.58) | data formatting | bytes 4194304
  98.7 40.0 %reduce-scatter.2.cloned.1.call-done = bf16[16,6144]{1,0:T(8,128)(2,1)} async-done(((bf16[128,6144]{1,0:T(8,128)(2,1)}), bf16[16,6144]{1,0:T(8,128)(2,1)}) %reduce-scatter.2.cloned.1.call-update) | async-done | bytes 196624 | tf_op jit(solution)/shard_map/reduce_scatter | solution.py:91
  138.7 1.7 reshape.112
  140.4 5.7 %all-to-all-start.1 = ((bf16[4,4,6144]{2,1,0:T(4,128)(2,1)}), bf16[4,4,6144]{2,1,0:T(4,128)(2,1)S(1)}, u32[]{:S(2)}, u32[]{:S(2)}) async-start(bf16[4,4,6144]{2,1,0:T(4,128)(2,1)} %reshape.112), calls=%async_computation.2 | async-start | bytes 393216 | tf_op jit(solution)/shard_map/all_to_all | solution.py:98
  146.2 10.7 %fusion.11 = f32[16,512,128]{1,2,0:T(8,128)} fusion(bf16[512,16,128]{0,2,1:T(8,128)(2,1)} %bitcast.65, bf16[512,16,128]{0,2,1:T(8,128)(2,1)S(1)} %bitcast.60, bf16[512,16,128]{0,2,1:T(8,128)(2,1)} %bitcast.63, f32[16,512]{1,0:T(8,128)S(1)} %get-tuple-element.63, pred[512,512]{1,0:T(8,128)(4,1)S(1)} %iota_compare_fusion), kind=kOutput, calls=%fused_computation.19 | convolution fusion | flops 2164260864 | bytes 10780672 | tf_op jit(solution)/shard_map/htu,uhd->thd/dot_general | solution.py:54
  157.0 13.0 %all-gather.1 = bf16[8,1,16]{2,1,0:T(2,128)(2,1)S(1)} all-gather(bf16[1,1,16]{2,1,0:T(2,128)(2,1)S(1)} %bitcast.68), channel_id=1, replica_groups=mesh['seq'=8,'exp'=4] {'seq'}, dimensions={0}, use_global_device_ids=true | all-gather | bytes 288 | tf_op jit(solution)/shard_map/all_gather | solution.py:14
  171.9 42.6 %all-gather.7.cloned.1.call-done = bf16[128,128,128]{2,1,0:T(8,128)(2,1)} async-done(((bf16[16,128,128]{2,1,0:T(8,128)(2,1)}), bf16[128,128,128]{2,1,0:T(8,128)(2,1)}) %all-gather.7.cloned.1.call-update) | async-done | bytes 4194320 | tf_op jit(solution)/shard_map/all_gather | solution.py:14
  214.6 9.4 %while.12 = (s32[]{:T(128)}, f32[16,128,128]{2,1,0:T(8,128)S(1)}, s32[]{:T(128)}, bf16[8,16]{1,0:T(8,128)(2,1)S(1)}, bf16[8,16,128,128]{3,2,1,0:T(8,128)(2,1)}, /*index=5*/s32[]{:T(128)}, s32[]{:T(128)}, s32[]{:T(128)}) while((s32[]{:T(128)}, f32[16,128,128]{2,1,0:T(8,128)S(1)}, s32[]{:T(128)}, bf16[8,16]{1,0:T(8,128)(2,1)S(1)}, ...), condition=%wide.region_3.4_spmd, body=%wide.region_2.3_spmd.sunk | while | flops 786453 | bytes 2621727 | solution.py:28
  214.6 1.3 convert_add_fusion.2
  216.0 1.3 convert_add_fusion.2
  217.3 1.3 convert_add_fusion.2
  218.7 1.3 convert_add_fusion.2
  224.0 5.8 %multiply_reduce_fusion = (f32[512,16]{0,1:T(8,128)S(1)}, f32[512,16,128]{0,2,1:T(8,128)S(1)}) fusion(f32[16,128,128]{2,1,0:T(8,128)S(1)} %get-tuple-element.46, bf16[512,16,128]{0,2,1:T(8,128)(2,1)S(1)} %bitcast.61, f32[512,16]{0,1:T(8,128)S(1)} %get-tuple-element.60, f32[16,512,128]{1,2,0:T(8,128)} %fusion.11), kind=kOutput, calls=%fused_computation.9 | convolution fusion | flops 1615847424 | bytes 11599872 | tf_op jit(solution)/shard_map/thd,hde->the/dot_general | solution.py:55
  229.8 2.5 %broadcast_multiply_fusion = f32[512,16,128]{0,2,1:T(8,128)} fusion(f32[512,16,128]{0,2,1:T(8,128)S(1)} %get-tuple-element.65, f32[512,16]{0,1:T(8,128)S(1)} %add_rsqrt_fusion), kind=kLoop, calls=%fused_computation.16 | loop fusion | flops 1048576 | bytes 8421376 | tf_op jit(solution)/shard_map/mul | solution.py:62
  232.3 5.4 %copy.65 = f32[512,2048]{1,0:T(8,128)} copy(f32[512,2048]{0,1:T(8,128)} %bitcast.58) | data formatting | bytes 8388608 | tf_op jit(solution)/shard_map/reshape | solution.py:63
  237.8 4.0 %multiply_convert_fusion.1 = bf16[512,2048]{1,0:T(8,128)(2,1)} fusion(f32[512,2048]{1,0:T(8,128)} %copy.65, f32[2048]{0:T(1024)S(1)} %copy-done.2), kind=kLoop, calls=%fused_computation.8 | loop fusion | flops 2097152 | bytes 6299648 | tf_op jit(solution)/shard_map/convert_element_type | solution.py:63
  (55 shorter events, 11.3 us)
Async XLA Ops:
  7.2 69.3 %copy-start = (f32[512,16]{0,1:T(8,128)S(1)}, f32[512,16]{0,1:T(8,128)}, u32[]{:S(2)}) copy-start(f32[512,16]{0,1:T(8,128)} %param.11) | copy-start | bytes 98308
  7.2 53.4 %all-gather.5.cloned.1.call-start = ((), (), s32[]{:S(2)}) async-start(), calls=%async_computation.3 | async-start | bytes 1769472 | tf_op jit(solution)/shard_map/all_gather | solution.py:86
  17.1 121.7 %reduce-scatter.2.cloned.1.call-start = ((), (), s32[]{:S(2)}) async-start(), calls=%async_computation.4 | async-start | bytes 1769472 | tf_op jit(solution)/shard_map/reduce_scatter | solution.py:91
  76.4 138.1 %all-gather.7.cloned.1.call-start = ((), (), s32[]{:S(2)}) async-start(), calls=%async_computation.5 | async-start | bytes 4718592 | tf_op jit(solution)/shard_map/all_gather | solution.py:14
  140.4 29.8 %all-to-all-start.1 = ((bf16[4,4,6144]{2,1,0:T(4,128)(2,1)}), bf16[4,4,6144]{2,1,0:T(4,128)(2,1)S(1)}, u32[]{:S(2)}, u32[]{:S(2)}) async-start(bf16[4,4,6144]{2,1,0:T(4,128)(2,1)} %reshape.112), calls=%async_computation.2 | async-start | bytes 393216 | tf_op jit(solution)/shard_map/all_to_all | solution.py:98
  146.2 23.9 %copy-start.3 = (f32[8,2]{0,1:T(2,128)S(1)}, f32[8,2]{0,1:T(2,128)}, u32[]{:S(2)}) copy-start(f32[8,2]{0,1:T(2,128)} %param.15) | copy-start | bytes 196
  232.3 5.4 %copy-start.2 = (f32[2048]{0:T(1024)S(1)}, f32[2048]{0:T(1024)}, u32[]{:S(2)}) copy-start(f32[2048]{0:T(1024)} %param.12) | copy-start | bytes 24580
  232.3 9.4 %copy-start.1 = (f32[512,16]{0,1:T(8,128)S(1)}, f32[512,16]{0,1:T(8,128)}, u32[]{:S(2)}) copy-start(f32[512,16]{0,1:T(8,128)} %param.11) | copy-start | bytes 98308
Sparse Core Ops, SparseCore 0:
  17.2 43.3 all-gather.4
  76.5 62.1 reduce-scatter.1
  141.1 73.3 all-gather.6
where the time goes:
time: 249 us; the launch traced here: 248 us
  waiting for transfers between devices  126 us (51%)
  matrix products  37.9 us (15%)
  local copies, waits for them, and re-layouts  25.9 us (10%)
  blocking collectives  19.6 us (8%)
  other arithmetic  18.7 us (8%)
  between operations  13.9 us (6%)
  starting transfers between devices  5.84 us (2%)
    all_gather x1, waiting for transfers between devices, on_device(): lax.all_gather(arrived.reshape(experts * CAP, model_width), 'seq', axis=0...  43.5 us
    all_gather x1, waiting for transfers between devices, prefix(): lax.all_gather(a.astype(kind), axis)  42.6 us
    reduce_scatter x1, waiting for transfers between devices, on_device(): lax.psum_scatter(jnp.dot(hidden, down, preferred_element_type=jnp.float32...  40 us
    all_gather x1, blocking collectives, prefix(): lax.all_gather(a.astype(kind), axis)  13 us
    dot_general x1, matrix products, on_device(): jnp.einsum('htu,uhd->thd', weights, values, preferred_element_type=jnp.fl...  10.7 us
    dot_general x1, matrix products, on_device(): jnp.dot(lax.all_gather(arrived.reshape(experts * CAP, model_width), 'seq'...  10.1 us
    add x7, other arithmetic, combine_states(): later[0][:, None, None] * earlier[1] + later[1]  9.08 us
    unnamed x13, local copies, waits for them, and re-layouts  7.68 us
  transfers between devices with their start and end apart: 4, of which 3 were waited for; matrix products, arithmetic and copies ran while one was open for 15% of the time, Pallas kernels for 0%

commit v1 on v0

--- a/solution.py
+++ b/solution.py
@@ -6,6 +6,18 @@
 CAP = 4
 EPS = 1e-06
 HIGH = lax.Precision.HIGHEST
+
+
+def gather_by_bits(x, axis, dim):
+    ways, here, step = (lax.axis_size(axis), lax.axis_index(axis), x.shape[dim])
+    line, have = (x, 1)
+    while have < ways:
+        line = jnp.concatenate(
+            [line, lax.ppermute(line, axis, [(d, (d - have) % ways) for d in range(ways)])],
+            axis=dim,
+        )
+        have = 2 * have
+    return jnp.roll(line, here * step, axis=dim)
 
 
 def prefix(shard, axis, join, neutral):
@@ -83,7 +95,7 @@
     )
     arrived = lax.all_to_all(outgoing, "exp", split_axis=0, concat_axis=0, tiled=True)
     both = jnp.dot(
-        lax.all_gather(arrived.reshape(experts * CAP, model_width), "seq", axis=0, tiled=True),
+        gather_by_bits(arrived.reshape(experts * CAP, model_width), "seq", 0),
         joined_in,
         preferred_element_type=jnp.float32,
     )

time: 249 us -> 260 us (1.044)
  waiting for transfers between devices: 126 us -> 137 us
    ppermute x0 -> x3, waiting for transfers between devices: none -> 54.3 us  [gather_by_bits(): lax.ppermute(line, axis, [(d, (d - have) % ways) for d in range(ways)])]
    all_gather x1 -> x0, waiting for transfers between devices: 43.5 us -> none  [on_device(): lax.all_gather(arrived.reshape(experts * CAP, model_width), 'seq', axis=0...]
    unnamed x13 -> x20, local copies, waits for them, and re-layouts: 7.68 us -> 6.41 us
  transfers between devices with their start and end apart: 4 -> 6, of which waited for: 3 -> 5; matrix products, arithmetic and copies ran while one was open for 15% -> 14% of each run, Pallas kernels for 0% -> 0%
where the time goes in v1:
time: 260 us; the launch traced here: 259 us
  waiting for transfers between devices  137 us (53%)
  matrix products  37.5 us (14%)
  local copies, waits for them, and re-layouts  25.4 us (10%)
  blocking collectives  19.6 us (8%)
  other arithmetic  18.8 us (7%)
  between operations  14.3 us (6%)
  starting transfers between devices  6.19 us (2%)
    ppermute x3, waiting for transfers between devices, gather_by_bits(): lax.ppermute(line, axis, [(d, (d - have) % ways) for d in range(ways)])  54.3 us
    all_gather x1, waiting for transfers between devices, prefix(): lax.all_gather(a.astype(kind), axis)  42.6 us
    reduce_scatter x1, waiting for transfers between devices, on_device(): lax.psum_scatter(jnp.dot(hidden, down, preferred_element_type=jnp.float32...  40.3 us
    all_gather x1, blocking collectives, prefix(): lax.all_gather(a.astype(kind), axis)  13.1 us
    dot_general x1, matrix products, on_device(): jnp.einsum('htu,uhd->thd', weights, values, preferred_element_type=jnp.fl...  10.7 us
    dot_general x1, matrix products, on_device(): jnp.dot(gather_by_bits(arrived.reshape(experts * CAP, model_width), 'seq'...  9.64 us
    add x7, other arithmetic, combine_states(): later[0][:, None, None] * earlier[1] + later[1]  9.08 us
    all_to_all x1, blocking collectives, on_device(): lax.all_to_all(outgoing, 'exp', split_axis=0, concat_axis=0, tiled=True)  6.58 us
  transfers between devices with their start and end apart: 6, of which 5 were waited for; matrix products, arithmetic and copies ran while one was open for 14% of the time, Pallas kernels for 0%

profile of v1, /device:TPU:31, one launch (start us, length us, event | category | flops | bytes accessed | tf_op | source)
XLA Modules:
  0.0 259.3 jit_solution(13140699687530710543)
XLA Ops:
  9.7 6.6 %all_to_all.10 = bf16[4,4,6144]{2,1,0:T(4,128)(2,1)S(1)} all-to-all(bf16[4,4,6144]{2,1,0:T(4,128)(2,1)S(1)} %reshape.109), channel_id=1, replica_groups=mesh['seq'=8,'exp'=4] {'exp'}, dimensions={0} | all-to-all | bytes 393216 | tf_op jit(solution)/shard_map/all_to_all | solution.py:96
  16.7 8.0 %collective-permute-done = bf16[16,6144]{1,0:T(8,128)(2,1)S(1)} collective-permute-done((bf16[16,6144]{1,0:T(8,128)(2,1)S(1)}, bf16[16,6144]{1,0:T(8,128)(2,1)S(1)}, u32[]{:S(2)}, u32[]{:S(2)}) %collective-permute-start) | collective-permute-done | bytes 196640 | tf_op jit(solution)/shard_map/ppermute | solution.py:16
  24.8 10.6 %collective-permute-done.1 = bf16[32,6144]{1,0:T(8,128)(2,1)S(1)} collective-permute-done((bf16[32,6144]{1,0:T(8,128)(2,1)S(1)}, bf16[32,6144]{1,0:T(8,128)(2,1)S(1)}, u32[]{:S(2)}, u32[]{:S(2)}) %collective-permute-start.1) | collective-permute-done | bytes 393248 | tf_op jit(solution)/shard_map/ppermute | solution.py:16
  35.6 35.7 %collective-permute-done.2 = bf16[64,6144]{1,0:T(8,128)(2,1)S(1)} collective-permute-done((bf16[64,6144]{1,0:T(8,128)(2,1)S(1)}, bf16[64,6144]{1,0:T(8,128)(2,1)S(1)}, u32[]{:S(2)}, u32[]{:S(2)}) %collective-permute-start.2) | collective-permute-done | bytes 786464 | tf_op jit(solution)/shard_map/ppermute | solution.py:16
  71.5 9.6 %fusion.12 = f32[128,1152]{1,0:T(8,128)S(1)} fusion(bf16[6144,1152]{0,1:T(8,128)(2,1)} %bitcast.58, bf16[256,6144]{1,0:T(8,128)(2,1)S(1)} %constant_dynamic-update-slice_fusion, s32[]{:T(128)S(6)} %select_n.26), kind=kOutput, calls=%fused_computation.20 | convolution fusion | flops 1811939328 | bytes 16318468 | tf_op jit(solution)/shard_map/dot_general | solution.py:97
  81.1 5.7 %convolution_convert_fusion = bf16[128,6144]{1,0:T(8,128)(2,1)} fusion(bf16[1,576,6144]{2,1,0:T(8,128)(2,1)} %param.17, f32[128,1152]{1,0:T(8,128)S(1)} %fusion.12), kind=kOutput, calls=%fused_computation.3 | convolution fusion | flops 907198464 | bytes 9306112 | tf_op jit(solution)/shard_map/dot_general | solution.py:104
  88.2 5.9 %fusion.28 = (bf16[512,1,2048]{2,0,1:T(8,128)(2,1)S(1)}, bf16[512,1,2048]{2,0,1:T(8,128)(2,1)}, bf16[512,1,2048]{2,0,1:T(8,128)(2,1)}) fusion(bf16[512,3,2048]{2,0,1:T(8,128)(2,1)} %param.10), kind=kLoop, calls=%fused_computation.59 | loop fusion | bytes 12582912 | tf_op jit(solution)/shard_map/slice | solution.py:52
  94.1 3.9 %copy.61 = bf16[512,1,2048]{0,2,1:T(8,128)(2,1)} copy(bf16[512,1,2048]{2,0,1:T(8,128)(2,1)} %get-tuple-element.59) | data formatting | bytes 4194304 | tf_op jit(solution)/shard_map/slice | solution.py:53
  98.0 2.5 copy.75
  100.9 5.3 %fusion.14 = bf16[16,128,128]{2,1,0:T(8,128)(2,1)} fusion(bf16[512,16,128]{0,2,1:T(8,128)(2,1)} %bitcast.61, bf16[512,16,128]{0,2,1:T(8,128)(2,1)} %bitcast.63, f32[512,16]{0,1:T(8,128)S(1)} %get-tuple-element.61), kind=kOutput, calls=%fused_computation.22 | convolution fusion | flops 1612972032 | bytes 4751360 | tf_op jit(solution)/shard_map/thi,thj->hij/dot_general | solution.py:57
  106.2 2.9 %copy.74 = bf16[512,1,2048]{0,2,1:T(8,128)(2,1)S(1)} copy(bf16[512,1,2048]{2,0,1:T(8,128)(2,1)} %get-tuple-element.58) | data formatting | bytes 4194304
  109.2 40.3 %reduce-scatter.2.cloned.1.call-done = bf16[16,6144]{1,0:T(8,128)(2,1)} async-done(((bf16[128,6144]{1,0:T(8,128)(2,1)}), bf16[16,6144]{1,0:T(8,128)(2,1)}) %reduce-scatter.2.cloned.1.call-update) | async-done | bytes 196624 | tf_op jit(solution)/shard_map/reduce_scatter | solution.py:103
  149.5 1.7 reshape.112
  151.2 5.7 %all-to-all-start.1 = ((bf16[4,4,6144]{2,1,0:T(4,128)(2,1)}), bf16[4,4,6144]{2,1,0:T(4,128)(2,1)S(1)}, u32[]{:S(2)}, u32[]{:S(2)}) async-start(bf16[4,4,6144]{2,1,0:T(4,128)(2,1)} %reshape.112), calls=%async_computation.2 | async-start | bytes 393216 | tf_op jit(solution)/shard_map/all_to_all | solution.py:110
  156.9 10.7 %fusion.11 = f32[16,512,128]{1,2,0:T(8,128)} fusion(bf16[512,16,128]{0,2,1:T(8,128)(2,1)} %bitcast.62, bf16[512,16,128]{0,2,1:T(8,128)(2,1)S(1)} %bitcast.59, bf16[512,16,128]{0,2,1:T(8,128)(2,1)} %bitcast.64, f32[16,512]{1,0:T(8,128)S(1)} %get-tuple-element.63, pred[512,512]{1,0:T(8,128)(4,1)S(1)} %iota_compare_fusion), kind=kOutput, calls=%fused_computation.19 | convolution fusion | flops 2164260864 | bytes 10780672 | tf_op jit(solution)/shard_map/htu,uhd->thd/dot_general | solution.py:66
  167.7 13.1 %all-gather.1 = bf16[8,1,16]{2,1,0:T(2,128)(2,1)S(1)} all-gather(bf16[1,1,16]{2,1,0:T(2,128)(2,1)S(1)} %bitcast.67), channel_id=1, replica_groups=mesh['seq'=8,'exp'=4] {'seq'}, dimensions={0}, use_global_device_ids=true | all-gather | bytes 288 | tf_op jit(solution)/shard_map/all_gather | solution.py:26
  182.7 42.6 %all-gather.4.cloned.1.call-done = bf16[128,128,128]{2,1,0:T(8,128)(2,1)} async-done(((bf16[16,128,128]{2,1,0:T(8,128)(2,1)}), bf16[128,128,128]{2,1,0:T(8,128)(2,1)}) %all-gather.4.cloned.1.call-update) | async-done | bytes 4194320 | tf_op jit(solution)/shard_map/all_gather | solution.py:26
  225.3 9.4 %while.12 = (s32[]{:T(128)}, f32[16,128,128]{2,1,0:T(8,128)S(1)}, s32[]{:T(128)}, bf16[8,16]{1,0:T(8,128)(2,1)S(1)}, bf16[8,16,128,128]{3,2,1,0:T(8,128)(2,1)}, /*index=5*/s32[]{:T(128)}, s32[]{:T(128)}, s32[]{:T(128)}) while((s32[]{:T(128)}, f32[16,128,128]{2,1,0:T(8,128)S(1)}, s32[]{:T(128)}, bf16[8,16]{1,0:T(8,128)(2,1)S(1)}, ...), condition=%wide.region_3.4_spmd, body=%wide.region_2.3_spmd.sunk | while | flops 786453 | bytes 2621735 | solution.py:40
  225.4 1.3 convert_add_fusion.2
  226.7 1.3 convert_add_fusion.2
  234.7 5.8 %multiply_reduce_fusion = (f32[512,16]{0,1:T(8,128)S(1)}, f32[512,16,128]{0,2,1:T(8,128)S(1)}) fusion(f32[16,128,128]{2,1,0:T(8,128)S(1)} %get-tuple-element.46, bf16[512,16,128]{0,2,1:T(8,128)(2,1)S(1)} %bitcast.60, f32[512,16]{0,1:T(8,128)S(1)} %get-tuple-element.60, f32[16,512,128]{1,2,0:T(8,128)} %fusion.11), kind=kOutput, calls=%fused_computation.9 | convolution fusion | flops 1615847424 | bytes 11599872 | tf_op jit(solution)/shard_map/thd,hde->the/dot_general | solution.py:67
  240.5 2.5 broadcast_multiply_fusion
  243.0 5.4 %copy.65 = f32[512,2048]{1,0:T(8,128)} copy(f32[512,2048]{0,1:T(8,128)} %bitcast.57) | data formatting | bytes 8388608 | tf_op jit(solution)/shard_map/reshape | solution.py:75
  248.5 4.0 %multiply_convert_fusion.1 = bf16[512,2048]{1,0:T(8,128)(2,1)} fusion(f32[512,2048]{1,0:T(8,128)} %copy.65, f32[2048]{0:T(1024)S(1)} %copy-done.2), kind=kLoop, calls=%fused_computation.8 | loop fusion | flops 2097152 | bytes 6299648 | tf_op jit(solution)/shard_map/convert_element_type | solution.py:75
  (68 shorter events, 13.8 us)
Async XLA Ops:
  7.2 79.7 %copy-start = (f32[512,16]{0,1:T(8,128)S(1)}, f32[512,16]{0,1:T(8,128)}, u32[]{:S(2)}) copy-start(f32[512,16]{0,1:T(8,128)} %param.11) | copy-start | bytes 98308
  7.2 142.3 %reduce-scatter.2.cloned.1.call-start = ((), (), s32[]{:S(2)}) async-start(), calls=%async_computation.3 | async-start | bytes 1769472 | tf_op jit(solution)/shard_map/reduce_scatter | solution.py:103
  16.4 8.3 %collective-permute-start = (bf16[16,6144]{1,0:T(8,128)(2,1)S(1)}, bf16[16,6144]{1,0:T(8,128)(2,1)S(1)}, u32[]{:S(2)}, u32[]{:S(2)}) collective-permute-start(bf16[16,6144]{1,0:T(8,128)(2,1)S(1)} %reshape.110), channel_id=1, source_target_pairs={{0,28},{4,0},{8,4},{12,8},{16,12},{20,16},{24,20},{28,24},{1,29},{... | collective-permute-start | bytes 589832 | tf_op jit(solution)/shard_map/ppermute | solution.py:16
  24.7 10.7 %collective-permute-start.1 = (bf16[32,6144]{1,0:T(8,128)(2,1)S(1)}, bf16[32,6144]{1,0:T(8,128)(2,1)S(1)}, u32[]{:S(2)}, u32[]{:S(2)}) collective-permute-start(bf16[32,6144]{1,0:T(8,128)(2,1)S(1)} %pad_maximum_fusion.1), channel_id=1, source_target_pairs={{0,24},{4,28},{8,0},{12,4},{16,8},{20,12},{24,16},{28,20},{1,25},{... | collective-permute-start | bytes 1179656 | tf_op jit(solution)/shard_map/ppermute | solution.py:16
  35.5 35.8 %collective-permute-start.2 = (bf16[64,6144]{1,0:T(8,128)(2,1)S(1)}, bf16[64,6144]{1,0:T(8,128)(2,1)S(1)}, u32[]{:S(2)}, u32[]{:S(2)}) collective-permute-start(bf16[64,6144]{1,0:T(8,128)(2,1)S(1)} %pad_maximum_fusion), channel_id=1, source_target_pairs={{0,16},{4,20},{8,24},{12,28},{16,0},{20,4},{24,8},{28,12},{1,17},{... | collective-permute-start | bytes 2359304 | tf_op jit(solution)/shard_map/ppermute | solution.py:16
  86.8 138.4 %all-gather.4.cloned.1.call-start = ((), (), s32[]{:S(2)}) async-start(), calls=%async_computation.4 | async-start | bytes 4718592 | tf_op jit(solution)/shard_map/all_gather | solution.py:26
  151.2 29.8 %all-to-all-start.1 = ((bf16[4,4,6144]{2,1,0:T(4,128)(2,1)}), bf16[4,4,6144]{2,1,0:T(4,128)(2,1)S(1)}, u32[]{:S(2)}, u32[]{:S(2)}) async-start(bf16[4,4,6144]{2,1,0:T(4,128)(2,1)} %reshape.112), calls=%async_computation.2 | async-start | bytes 393216 | tf_op jit(solution)/shard_map/all_to_all | solution.py:110
  156.9 23.9 %copy-start.3 = (f32[8,2]{0,1:T(2,128)S(1)}, f32[8,2]{0,1:T(2,128)}, u32[]{:S(2)}) copy-start(f32[8,2]{0,1:T(2,128)} %param.15) | copy-start | bytes 196
  243.0 5.4 %copy-start.2 = (f32[2048]{0:T(1024)S(1)}, f32[2048]{0:T(1024)}, u32[]{:S(2)}) copy-start(f32[2048]{0:T(1024)} %param.12) | copy-start | bytes 24580
  243.0 9.4 %copy-start.1 = (f32[512,16]{0,1:T(8,128)S(1)}, f32[512,16]{0,1:T(8,128)}, u32[]{:S(2)}) copy-start(f32[512,16]{0,1:T(8,128)} %param.11) | copy-start | bytes 98308
Sparse Core Ops, SparseCore 0:
  86.9 62.5 reduce-scatter.1
  151.8 73.3 all-gather.3
